TPU v7x, 32 devices: a whole 2x2x4 slice. The times are simulated.
32 devices in a mesh: groups: 2 (over y), row: 8 (over z, x), section: 2 (over core).
Axes of the slice: x: 2, y: 2, z: 4, core: 2. Of those that a mesh axis runs over, the one named last changes fastest.
Arguments:
- hidden: bfloat16 [64, 8192], P('groups', ('row', 'section')), parts along dimension 0, may hold values from -6 to 6
- norm_in_gain: float32 [8192], replicated, may hold values from 0.1 to 1.9
- zx_weight: bfloat16 [8192, 2, 8, 64], P(None, None, 'row', 'section'), may hold values from -0.0625 to 0.0625
- bc_weight: bfloat16 [8192, 2048], P(None, ('row', 'section')), may hold values from -0.0625 to 0.0625
- dt_weight: bfloat16 [8192, 8], P(None, 'row'), may hold values from -0.0625 to 0.0625
- dt_bias: float32 [8], P('row'), may hold values from -3 to -0.5
- decay_log: float32 [8], P('row'), may hold values from -0.7 to 2
- skip_gain: float32 [8], P('row'), may hold values from 0.5 to 1.5
- conv_x_weight: float32 [4, 8, 64], P(None, 'row', 'section'), may hold values from -3.6 to 3.6
- conv_x_bias: float32 [8, 64], P('row', 'section'), may hold values from -3 to 3
- conv_bc_weight: float32 [4, 2048], P(None, ('row', 'section')), may hold values from -3 to 3
- conv_bc_bias: float32 [2048], P(('row', 'section')), may hold values from -3 to 3
- conv_x_state: bfloat16 [64, 3, 8, 64], P('groups', None, 'row', 'section'), parts along dimension 0, may hold values from -6 to 6
- conv_bc_state: bfloat16 [64, 3, 2048], P('groups', None, ('row', 'section')), parts along dimension 0, may hold values from -6 to 6
- ssm_state: bfloat16 [64, 8, 64, 256], P('groups', 'row', 'section'), parts along dimension 0, may hold values from -6 to 6
- gate_norm_weight: float32 [8, 64], P('row', 'section'), may hold values from 0.1 to 1.9
- out_weight: bfloat16 [8, 64, 8192], P('row', 'section'), may hold values from -0.375 to 0.375
- norm_mid_gain: float32 [8192], replicated, may hold values from 0.1 to 1.9
- up_weight: bfloat16 [8192, 16384], P(None, ('row', 'section')), may hold values from -0.0625 to 0.0625
- down_weight: bfloat16 [16384, 8192], P(('row', 'section')), may hold values from -0.0625 to 0.0625
- valid: int32 [64], P('groups'), parts along dimension 0, may hold values 0 or 1
Outputs:
- block_out: bfloat16 [64, 8192], P('groups', ('row', 'section')), parts along dimension 0
- new_ssm_state: bfloat16 [64, 8, 64, 256], P('groups', 'row', 'section'), parts along dimension 0
- new_conv_x_state: bfloat16 [64, 3, 8, 64], P('groups', None, 'row', 'section'), parts along dimension 0
- new_conv_bc_state: bfloat16 [64, 3, 2048], P('groups', None, ('row', 'section')), parts along dimension 0
There are 2 independent parts, one for each index of `groups`. A program takes and returns all parts, laid end to end along the dimension named above; an argument that names none is the same for every part. Nothing has to cross between parts.
All inputs are finite; a program needn't handle non-finite values.
Results may differ from a plain program's by a relative error of at most 0.0075.
Values may be sent and summed in bfloat16 or wider, within the bound.
A program may use at most 128 MiB of HBM per device.

v0:
```python
import jax
import jax.numpy as jnp
from jax import lax
from jax.sharding import PartitionSpec as P

D = 8192
HEAD_DIM = 64
STATE = 256
GROUPS = 4


def mean_norm(values, gain):
    return values * lax.rsqrt(jnp.mean(values * values, axis=-1, keepdims=True) + 1e-05) * gain


def body(
    hidden,
    norm_in_gain,
    zx_weight,
    bc_weight,
    dt_weight,
    dt_bias,
    decay_log,
    skip_gain,
    conv_x_weight,
    conv_x_bias,
    conv_bc_weight,
    conv_bc_bias,
    conv_x_state,
    conv_bc_state,
    ssm_state,
    gate_norm_weight,
    out_weight,
    norm_mid_gain,
    up_weight,
    down_weight,
    valid,
):
    row_count = hidden.shape[0]
    local_p = zx_weight.shape[3]
    full_rows = lax.all_gather(hidden, ("row", "section"), axis=1, tiled=True)
    normed = mean_norm(full_rows.astype(jnp.float32), norm_in_gain).astype(jnp.bfloat16)
    gate_inner = jnp.dot(
        normed, zx_weight.reshape(D, 2 * local_p), preferred_element_type=jnp.float32
    ).reshape(row_count, 2, 1, local_p)
    gate_part = gate_inner[:, 0]
    inner_pre = gate_inner[:, 1].astype(jnp.bfloat16)
    bc_pre = jnp.dot(normed, bc_weight, preferred_element_type=jnp.float32).astype(jnp.bfloat16)
    dt_raw = jnp.dot(normed, dt_weight, preferred_element_type=jnp.float32)
    taps_x = jnp.concatenate([conv_x_state, inner_pre[:, None]], axis=1)
    inner = jax.nn.silu(
        jnp.sum(taps_x.astype(jnp.float32) * conv_x_weight[None], axis=1) + conv_x_bias
    )
    taps_bc = jnp.concatenate([conv_bc_state, bc_pre[:, None]], axis=1)
    mixed_bc = jax.nn.silu(
        jnp.sum(taps_bc.astype(jnp.float32) * conv_bc_weight[None], axis=1) + conv_bc_bias
    )
    all_bc = lax.all_gather(mixed_bc, ("row", "section"), axis=1, tiled=True)
    per_group = lax.axis_size("row") // GROUPS
    group_index = lax.axis_index("row") // per_group
    state_in = all_bc[:, : GROUPS * STATE].reshape(row_count, GROUPS, STATE)
    state_out = all_bc[:, GROUPS * STATE :].reshape(row_count, GROUPS, STATE)
    in_mine = lax.dynamic_slice_in_dim(state_in, group_index, 1, axis=1)
    out_mine = lax.dynamic_slice_in_dim(state_out, group_index, 1, axis=1)
    step_size = jax.nn.softplus(dt_raw + dt_bias[None])
    decay_rate = jnp.exp(-step_size * jnp.exp(decay_log)[None])
    previous = ssm_state.astype(jnp.float32)
    updated = (
        decay_rate[:, :, None, None] * previous
        + (step_size[:, :, None] * inner)[..., None] * in_mine[:, :, None, :]
    )
    readout = (
        jnp.einsum("rhpn,rhn->rhp", updated, out_mine, precision=lax.Precision.HIGHEST)
        + skip_gain[None, :, None] * inner
    )
    gated = readout * jax.nn.silu(gate_part)
    local_squares = jnp.sum(gated * gated, axis=(1, 2))
    group_pick = (jnp.arange(GROUPS) == group_index).astype(jnp.float32)
    group_sums = lax.psum(local_squares[:, None] * group_pick[None], ("row", "section"))
    group_size = per_group * HEAD_DIM
    group_mean = jnp.sum(group_sums * group_pick[None], axis=1) / group_size
    scaled = (gated * lax.rsqrt(group_mean + 1e-05)[:, None, None] * gate_norm_weight[None]).astype(
        jnp.bfloat16
    )
    mixer_terms = jnp.dot(
        scaled.reshape(row_count, local_p),
        out_weight.reshape(local_p, D),
        preferred_element_type=jnp.float32,
    )
    mixer_share = lax.psum_scatter(mixer_terms, ("row", "section"), scatter_dimension=1, tiled=True)
    middle = (hidden.astype(jnp.float32) + mixer_share).astype(jnp.bfloat16)
    middle_full = lax.all_gather(middle, ("row", "section"), axis=1, tiled=True)
    mlp_in = mean_norm(middle_full.astype(jnp.float32), norm_mid_gain).astype(jnp.bfloat16)
    up_values = jnp.dot(mlp_in, up_weight, preferred_element_type=jnp.float32)
    activated = jnp.square(jax.nn.relu(up_values)).astype(jnp.bfloat16)
    down_terms = jnp.dot(activated, down_weight, preferred_element_type=jnp.float32)
    down_share = lax.psum_scatter(down_terms, ("row", "section"), scatter_dimension=1, tiled=True)
    block_out = (middle.astype(jnp.float32) + down_share).astype(jnp.bfloat16)
    kept_rows = valid != 0
    new_ssm_state = jnp.where(kept_rows[:, None, None, None], updated, previous).astype(
        jnp.bfloat16
    )
    new_conv_x_state = jnp.where(kept_rows[:, None, None, None], taps_x[:, 1:], conv_x_state)
    new_conv_bc_state = jnp.where(kept_rows[:, None, None], taps_bc[:, 1:], conv_bc_state)
    return (block_out, new_ssm_state, new_conv_x_state, new_conv_bc_state)


def solution(mesh):
    return jax.shard_map(
        body,
        mesh=mesh,
        in_specs=(
            P("groups", ("row", "section")),
            P(),
            P(None, None, "row", "section"),
            P(None, ("row", "section")),
            P(None, "row"),
            P("row"),
            P("row"),
            P("row"),
            P(None, "row", "section"),
            P("row", "section"),
            P(None, ("row", "section")),
            P(("row", "section")),
            P("groups", None, "row", "section"),
            P("groups", None, ("row", "section")),
            P("groups", "row", "section", None),
            P("row", "section"),
            P("row", "section", None),
            P(),
            P(None, ("row", "section")),
            P(("row", "section"), None),
            P("groups"),
        ),
        out_specs=(
            P("groups", ("row", "section")),
            P("groups", "row", "section", None),
            P("groups", None, "row", "section"),
            P("groups", None, ("row", "section")),
        ),
        check_vma=False,
    )
```

profile of v0, /device:TPU:0, one launch (start us, length us, event | category | flops | bytes accessed | tf_op | source)
XLA Modules:
  0.0 251.6 jit_solution(10273601416538449090)
XLA Ops:
  7.2 0.0 copy-start
  7.2 0.0 reduce-scatter.3.cloned.1.call-start
  7.3 24.9 %all_gather.9 = bf16[32,8192]{1,0:T(8,128)(2,1)S(1)} all-gather(bf16[32,512]{1,0:T(8,128)(2,1)} %param.21), channel_id=1, replica_groups=mesh['groups'=2,'row'=8,'section'=2] {'row','section'}, dimensions={1}, use_global_device_ids=true | all-gather | bytes 557056 | tf_op jit(solution)/shard_map/all_gather | solution.py:41
  32.2 0.2 fusion.4
  32.4 1.7 convolution_bitcast_fusion
  34.2 0.1 copy.32
  34.3 0.8 multiply_reduce_fusion.1
  35.0 0.1 copy.33
  35.8 0.0 copy-done
  35.8 1.2 fusion.2
  37.0 0.8 multiply_reduce_fusion
  37.8 0.7 divide_multiply_fusion
  38.4 18.1 %all_gather.10 = f32[32,2048]{1,0:T(8,128)S(1)} all-gather(f32[32,128]{1,0:T(8,128)S(1)} %divide_multiply_fusion), channel_id=1, replica_groups=mesh['groups'=2,'row'=8,'section'=2] {'row','section'}, dimensions={1}, use_global_device_ids=true | all-gather | bytes 278528 | tf_op jit(solution)/shard_map/all_gather | solution.py:58
  56.6 0.1 reshape.225
  58.1 1.1 multiply_exponential_fusion
  59.2 0.8 broadcast_multiply_fusion
  60.0 0.1 copy.34
  60.0 0.1 reshape.227
  60.1 2.3 fusion.13
  62.3 0.1 copy.36
  62.4 0.8 multiply_reduce_fusion.2
  63.2 0.1 broadcast_multiply_fusion.1
  63.3 31.1 %psum.7 = f32[32,4]{0,1:T(4,128)S(1)} all-reduce(f32[32,4]{0,1:T(4,128)S(1)} %broadcast_multiply_fusion.1), channel_id=1, replica_groups=mesh['groups'=2,'row'=8,'section'=2] {'row','section'}, use_global_device_ids=true, to_apply=%region_4.5 | all-reduce | flops 128 | bytes 1024 | tf_op jit(solution)/shard_map/psum | solution.py:79
  94.4 0.1 multiply_reduce_fusion.3
  94.5 2.5 fusion.19
  96.9 0.0 reduce-scatter.3.cloned.1.call-update
  96.9 0.0 reduce-scatter.5.cloned.1.call-start
  97.0 54.8 %reduce-scatter.3.cloned.1.call-done = f32[32,512]{1,0:T(8,128)} async-done(((f32[32,8192]{1,0:T(8,128)}), f32[32,512]{1,0:T(8,128)}) %reduce-scatter.3.cloned.1.call-update) | async-done | bytes 65552 | tf_op jit(solution)/shard_map/reduce_scatter | solution.py:90
  151.8 0.8 add_convert_fusion.1
  152.6 20.8 %all_gather.11 = bf16[32,8192]{1,0:T(8,128)(2,1)S(1)} all-gather(bf16[32,512]{1,0:T(8,128)(2,1)S(1)} %add_convert_fusion.1), channel_id=1, replica_groups=mesh['groups'=2,'row'=8,'section'=2] {'row','section'}, dimensions={1}, use_global_device_ids=true | all-gather | bytes 557056 | tf_op jit(solution)/shard_map/all_gather | solution.py:92
  173.5 0.2 fusion.9
  173.7 0.0 copy-start.4
  173.7 0.0 copy-start.2
  173.7 0.0 copy-start.3
  173.7 0.0 copy-start.1
  173.7 14.8 %fusion.16 = f32[32,8192]{1,0:T(8,128)} fusion(bf16[1024,8192]{1,0:T(8,128)(2,1)} %param.40, bf16[8192,1024]{1,0:T(8,128)(2,1)} %param.39, bf16[32,8192]{1,0:T(8,128)(2,1)S(1)} %all_gather.11, f32[8192]{0:T(1024)} %param.38, f32[32]{0:T(128)S(1)} %add_rsqrt_fusion), kind=kOutput, calls=%fused_computation.25 | convolution fusion | flops 1074888704 | bytes 35160192 | tf_op jit(solution)/shard_map/dot_general | solution.py:96
  188.5 0.0 reduce-scatter.5.cloned.1.call-update
  188.5 0.0 copy-done.4
  188.5 0.0 copy-done.2
  188.6 0.7 fusion.35
  189.2 0.0 copy-done.3
  189.2 0.7 fusion.33
  189.9 0.0 copy-done.1
  189.9 1.2 fusion.8
  191.1 52.2 %reduce-scatter.5.cloned.1.call-done = f32[32,512]{1,0:T(8,128)} async-done(((f32[32,8192]{1,0:T(8,128)}), f32[32,512]{1,0:T(8,128)}) %reduce-scatter.5.cloned.1.call-update) | async-done | bytes 65552 | tf_op jit(solution)/shard_map/reduce_scatter | solution.py:97
  243.3 1.5 add_convert_fusion
  (9 shorter events, 0.1 us)
Async XLA Ops:
  7.2 28.6 %copy-start = (bf16[8192,128]{1,0:T(8,128)(2,1)S(1)}, bf16[8192,128]{1,0:T(8,128)(2,1)}, u32[]{:S(2)}) copy-start(bf16[8192,128]{1,0:T(8,128)(2,1)} %param.24) | copy-start | bytes 6291460
  7.2 144.6 %reduce-scatter.3.cloned.1.call-start = ((), (), s32[]{:S(2)}) async-start(), calls=%async_computation.2 | async-start | bytes 1114112 | tf_op jit(solution)/shard_map/reduce_scatter | solution.py:90
  96.9 146.4 %reduce-scatter.5.cloned.1.call-start = ((), (), s32[]{:S(2)}) async-start(), calls=%async_computation.3 | async-start | bytes 1114112 | tf_op jit(solution)/shard_map/reduce_scatter | solution.py:97
  173.7 14.8 %copy-start.4 = (s32[32]{0:T(128)S(1)}, s32[32]{0:T(128)}, u32[]{:S(2)}) copy-start(s32[32]{0:T(128)} %param.41) | copy-start | bytes 388
  173.7 14.8 %copy-start.2 = (bf16[32,3,1,32]{3,0,2,1:T(8,128)(2,1)S(1)}, bf16[32,3,1,32]{3,0,2,1:T(8,128)(2,1)}, u32[]{:S(2)}) copy-start(bf16[32,3,1,32]{3,0,2,1:T(8,128)(2,1)} %param.33) | copy-start | bytes 18436
  173.7 15.5 %copy-start.3 = (bf16[32,3,128]{2,0,1:T(8,128)(2,1)S(1)}, bf16[32,3,128]{2,0,1:T(8,128)(2,1)}, u32[]{:S(2)}) copy-start(bf16[32,3,128]{2,0,1:T(8,128)(2,1)} %param.34) | copy-start | bytes 73732
  173.7 16.2 %copy-start.1 = (bf16[32,1,32,256]{3,2,1,0:T(8,128)(2,1)S(1)}, bf16[32,1,32,256]{3,2,1,0:T(8,128)(2,1)}, u32[]{:S(2)}) copy-start(bf16[32,1,32,256]{3,2,1,0:T(8,128)(2,1)} %param.35) | copy-start | bytes 1572868
Sparse Core Ops, SparseCore 0:
  97.1 54.6 reduce-scatter.2
  188.6 54.6 reduce-scatter.4
where the time goes:
time: 252 us
  waiting for transfers between devices  107 us (42%)
  blocking collectives  95 us (38%)
  matrix products  23.5 us (9%)
  between operations  16.2 us (6%)
  other arithmetic  9.25 us (4%)
    reduce_scatter x1, waiting for transfers between devices, body(): lax.psum_scatter(mixer_terms, ('row', 'section'), scatter_dimension=1, ti...  54.8 us
    reduce_scatter x1, waiting for transfers between devices, body(): lax.psum_scatter(down_terms, ('row', 'section'), scatter_dimension=1, til...  52.2 us
    psum x1, blocking collectives, body(): lax.psum(local_squares[:, None] * group_pick[None], ('row', 'section'))  31.1 us
    all_gather x1, blocking collectives, body(): full_rows = lax.all_gather(hidden, ('row', 'section'), axis=1, tiled=True)  24.9 us
    all_gather x1, blocking collectives, body(): middle_full = lax.all_gather(middle, ('row', 'section'), axis=1, tiled=True)  20.8 us
    all_gather x1, blocking collectives, body(): all_bc = lax.all_gather(mixed_bc, ('row', 'section'), axis=1, tiled=True)  18.1 us
    dot_general x1, matrix products, body(): jnp.dot(activated, down_weight, preferred_element_type=jnp.float32)  14.8 us
  transfers between devices with their start and end apart: 2, of which 2 were waited for; matrix products, arithmetic and copies ran while one was open for 1% of the time, Pallas kernels for 0%

commit v1 on v0

--- a/solution.py
+++ b/solution.py
@@ -76,7 +76,9 @@
     gated = readout * jax.nn.silu(gate_part)
     local_squares = jnp.sum(gated * gated, axis=(1, 2))
     group_pick = (jnp.arange(GROUPS) == group_index).astype(jnp.float32)
-    group_sums = lax.psum(local_squares[:, None] * group_pick[None], ("row", "section"))
+    group_sums = jnp.sum(
+        lax.all_gather(local_squares[:, None] * group_pick[None], ("row", "section")), axis=0
+    )
     group_size = per_group * HEAD_DIM
     group_mean = jnp.sum(group_sums * group_pick[None], axis=1) / group_size
     scaled = (gated * lax.rsqrt(group_mean + 1e-05)[:, None, None] * gate_norm_weight[None]).astype(

time: 252 us -> 240 us (0.952)
  blocking collectives: 95 us -> 82.8 us
    psum x1 -> x0, blocking collectives: 31.1 us -> none  [body(): lax.psum(local_squares[:, None] * group_pick[None], ('row', 'section'))]
    all_gather x0 -> x1, blocking collectives: none -> 18.8 us  [body(): lax.all_gather(local_squares[:, None] * group_pick[None], ('row', 'sectio...]
where the time goes in v1:
time: 240 us; the launch traced here: 239 us
  waiting for transfers between devices  107 us (45%)
  blocking collectives  82.8 us (34%)
  matrix products  23.5 us (10%)
  between operations  16.2 us (7%)
  other arithmetic  9.28 us (4%)
    reduce_scatter x1, waiting for transfers between devices, body(): lax.psum_scatter(mixer_terms, ('row', 'section'), scatter_dimension=1, ti...  54.8 us
    reduce_scatter x1, waiting for transfers between devices, body(): lax.psum_scatter(down_terms, ('row', 'section'), scatter_dimension=1, til...  52.2 us
    all_gather x1, blocking collectives, body(): full_rows = lax.all_gather(hidden, ('row', 'section'), axis=1, tiled=True)  24.9 us
    all_gather x1, blocking collectives, body(): middle_full = lax.all_gather(middle, ('row', 'section'), axis=1, tiled=True)  20.9 us
    all_gather x1, blocking collectives, body(): lax.all_gather(local_squares[:, None] * group_pick[None], ('row', 'sectio...  18.8 us
    all_gather x1, blocking collectives, body(): all_bc = lax.all_gather(mixed_bc, ('row', 'section'), axis=1, tiled=True)  18.1 us
    dot_general x1, matrix products, body(): jnp.dot(activated, down_weight, preferred_element_type=jnp.float32)  14.8 us
  transfers between devices with their start and end apart: 2, of which 2 were waited for; matrix products, arithmetic and copies ran while one was open for 1% of the time, Pallas kernels for 0%

profile of v1, /device:TPU:0, one launch (start us, length us, event | category | flops | bytes accessed | tf_op | source)
XLA Modules:
  0.0 239.4 jit_solution(13127866179666446147)
XLA Ops:
  7.2 0.0 copy-start
  7.2 0.0 reduce-scatter.3.cloned.1.call-start
  7.3 24.9 %all_gather.13 = bf16[32,8192]{1,0:T(8,128)(2,1)S(1)} all-gather(bf16[32,512]{1,0:T(8,128)(2,1)} %param.21), channel_id=1, replica_groups=mesh['groups'=2,'row'=8,'section'=2] {'row','section'}, dimensions={1}, use_global_device_ids=true | all-gather | bytes 557056 | tf_op jit(solution)/shard_map/all_gather | solution.py:41
  32.2 0.2 fusion.4
  32.4 1.7 convolution_bitcast_fusion
  34.2 0.1 copy.32
  34.3 0.8 multiply_reduce_fusion.1
  35.0 0.1 copy.33
  35.8 0.0 copy-done
  35.8 1.2 fusion.2
  37.0 0.8 multiply_reduce_fusion
  37.8 0.7 divide_multiply_fusion
  38.4 18.1 %all_gather.14 = f32[32,2048]{1,0:T(8,128)S(1)} all-gather(f32[32,128]{1,0:T(8,128)S(1)} %divide_multiply_fusion), channel_id=1, replica_groups=mesh['groups'=2,'row'=8,'section'=2] {'row','section'}, dimensions={1}, use_global_device_ids=true | all-gather | bytes 278528 | tf_op jit(solution)/shard_map/all_gather | solution.py:58
  56.6 0.1 reshape.266
  58.1 1.1 multiply_exponential_fusion
  59.2 0.8 broadcast_multiply_fusion
  60.0 0.1 copy.34
  60.0 0.1 reshape.268
  60.1 2.3 fusion.13
  62.3 0.1 copy.36
  62.4 0.8 multiply_reduce_fusion.2
  63.2 0.1 broadcast_multiply_fusion.1
  63.3 18.8 %all_gather.15 = f32[16,32,4]{1,2,0:T(4,128)S(1)} all-gather(f32[1,32,4]{1,2,0:T(4,128)S(1)} %broadcast_multiply_fusion.1), channel_id=1, replica_groups=mesh['groups'=2,'row'=8,'section'=2] {'row','section'}, dimensions={0}, use_global_device_ids=true | all-gather | bytes 8704 | tf_op jit(solution)/shard_map/all_gather | solution.py:80
  82.1 0.1 multiply_reduce_fusion.3
  82.2 2.4 %fusion.19 = f32[32,8192]{1,0:T(8,128)} fusion(bf16[1,32,8192]{2,1,0:T(8,128)(2,1)} %param.37, f32[32,32]{0,1:T(8,128)S(1)} %get-tuple-element.5, f32[32]{0:T(128)} %bitcast.59, f32[32]{0:T(128)S(1)} %add_rsqrt_fusion.1), kind=kOutput, calls=%fused_computation.26 | convolution fusion | flops 16780288 | bytes 1577216 | tf_op jit(solution)/shard_map/dot_general | solution.py:87
  84.7 0.0 reduce-scatter.3.cloned.1.call-update
  84.7 0.0 reduce-scatter.5.cloned.1.call-start
  84.8 54.8 %reduce-scatter.3.cloned.1.call-done = f32[32,512]{1,0:T(8,128)} async-done(((f32[32,8192]{1,0:T(8,128)}), f32[32,512]{1,0:T(8,128)}) %reduce-scatter.3.cloned.1.call-update) | async-done | bytes 65552 | tf_op jit(solution)/shard_map/reduce_scatter | solution.py:92
  139.6 0.8 add_convert_fusion.1
  140.4 20.9 %all_gather.16 = bf16[32,8192]{1,0:T(8,128)(2,1)S(1)} all-gather(bf16[32,512]{1,0:T(8,128)(2,1)S(1)} %add_convert_fusion.1), channel_id=1, replica_groups=mesh['groups'=2,'row'=8,'section'=2] {'row','section'}, dimensions={1}, use_global_device_ids=true | all-gather | bytes 557056 | tf_op jit(solution)/shard_map/all_gather | solution.py:94
  161.3 0.2 fusion.9
  161.5 0.0 copy-start.4
  161.5 0.0 copy-start.2
  161.5 0.0 copy-start.3
  161.5 0.0 copy-start.1
  161.6 14.8 %fusion.16 = f32[32,8192]{1,0:T(8,128)} fusion(bf16[1024,8192]{1,0:T(8,128)(2,1)} %param.40, bf16[8192,1024]{1,0:T(8,128)(2,1)} %param.39, bf16[32,8192]{1,0:T(8,128)(2,1)S(1)} %all_gather.16, f32[8192]{0:T(1024)} %param.38, f32[32]{0:T(128)S(1)} %add_rsqrt_fusion), kind=kOutput, calls=%fused_computation.25 | convolution fusion | flops 1074888704 | bytes 35160192 | tf_op jit(solution)/shard_map/dot_general | solution.py:98
  176.3 0.0 reduce-scatter.5.cloned.1.call-update
  176.3 0.0 copy-done.4
  176.4 0.0 copy-done.2
  176.4 0.7 fusion.35
  177.1 0.0 copy-done.3
  177.1 0.7 fusion.33
  177.7 0.0 copy-done.1
  177.8 1.2 fusion.8
  178.9 52.2 %reduce-scatter.5.cloned.1.call-done = f32[32,512]{1,0:T(8,128)} async-done(((f32[32,8192]{1,0:T(8,128)}), f32[32,512]{1,0:T(8,128)}) %reduce-scatter.5.cloned.1.call-update) | async-done | bytes 65552 | tf_op jit(solution)/shard_map/reduce_scatter | solution.py:99
  231.1 1.5 add_convert_fusion
  (10 shorter events, 0.1 us)
Async XLA Ops:
  7.2 28.6 %copy-start = (bf16[8192,128]{1,0:T(8,128)(2,1)S(1)}, bf16[8192,128]{1,0:T(8,128)(2,1)}, u32[]{:S(2)}) copy-start(bf16[8192,128]{1,0:T(8,128)(2,1)} %param.24) | copy-start | bytes 6291460
  7.2 132.4 %reduce-scatter.3.cloned.1.call-start = ((), (), s32[]{:S(2)}) async-start(), calls=%async_computation.2 | async-start | bytes 1114112 | tf_op jit(solution)/shard_map/reduce_scatter | solution.py:92
  84.7 146.4 %reduce-scatter.5.cloned.1.call-start = ((), (), s32[]{:S(2)}) async-start(), calls=%async_computation.3 | async-start | bytes 1114112 | tf_op jit(solution)/shard_map/reduce_scatter | solution.py:99
  161.5 14.8 %copy-start.4 = (s32[32]{0:T(128)S(1)}, s32[32]{0:T(128)}, u32[]{:S(2)}) copy-start(s32[32]{0:T(128)} %param.41) | copy-start | bytes 388
  161.5 14.8 %copy-start.2 = (bf16[32,3,1,32]{3,0,2,1:T(8,128)(2,1)S(1)}, bf16[32,3,1,32]{3,0,2,1:T(8,128)(2,1)}, u32[]{:S(2)}) copy-start(bf16[32,3,1,32]{3,0,2,1:T(8,128)(2,1)} %param.33) | copy-start | bytes 18436
  161.5 15.5 %copy-start.3 = (bf16[32,3,128]{2,0,1:T(8,128)(2,1)S(1)}, bf16[32,3,128]{2,0,1:T(8,128)(2,1)}, u32[]{:S(2)}) copy-start(bf16[32,3,128]{2,0,1:T(8,128)(2,1)} %param.34) | copy-start | bytes 73732
  161.5 16.2 %copy-start.1 = (bf16[32,1,32,256]{3,2,1,0:T(8,128)(2,1)S(1)}, bf16[32,1,32,256]{3,2,1,0:T(8,128)(2,1)}, u32[]{:S(2)}) copy-start(bf16[32,1,32,256]{3,2,1,0:T(8,128)(2,1)} %param.35) | copy-start | bytes 1572868
Sparse Core Ops, SparseCore 0:
  84.8 54.6 reduce-scatter.2
  176.5 54.5 reduce-scatter.4
